TPU v7x, 256 devices: a whole 4x4x8 slice. The times are simulated.
256 devices in a mesh: lat: 16 (over y_hi, z), lon: 8 (over y_lo, x), head: 2 (over core).
Axes of the slice: x: 4, y: 4 (y_hi: 2, y_lo: 2; y = y_hi * 2 + y_lo), z: 8, core: 2. Of those that a mesh axis runs over, the one named last changes fastest.
Arguments:
- queries: bfloat16 [16, 8, 512, 1024], P('lat', 'lon', None, 'head'), may hold values from -250 to 250, as said below
- key_value: bfloat16 [16, 8, 512, 128], P('lat', 'lon'), may hold values from -5 to 5
- dout: bfloat16 [16, 8, 512, 1024], P('lat', 'lon', None, 'head'), may hold values from -6 to 6
Outputs:
- dquery: bfloat16 [16, 8, 512, 1024], P('lat', 'lon', None, 'head')
- dkey_value: float32 [16, 8, 512, 128], P('lat', 'lon', 'head')
Inputs may be any that keep to these rules, and one draw needn't show every extreme that they name: `queries`: queries and keys have entries of order one, except that some query rows may be large multiples of nearby keys.
All inputs are finite; a program needn't handle non-finite values.
Results may differ from a plain program's by a relative error of at most 0.005.
Values may be sent and summed in bfloat16 or wider, within the bound.
No kernel may reach another device: no remote copies, remote signals or barrier semaphores. Data moves between devices by JAX's collectives and lax.ppermute only.
A program may use at most 64 MiB of HBM per device.

v0:
```python
import jax
import jax.numpy as jnp
from jax import lax
from jax.sharding import PartitionSpec as P

HEAD_DIM = 64


def passed_along(array, axis, by):
    peers = lax.axis_size(axis)
    return lax.ppermute(array, axis, [(i, (i + by) % peers) for i in range(peers)])


def gather_near(tile):
    pieces = []
    for step in (-2, 2):
        pieces.append(passed_along(tile, "lat", step))
    for step in (-2, 2):
        pieces.append(passed_along(tile, "lon", step))
    return jnp.stack(pieces)


def send_back(parts):
    total = parts[0]
    offsets = (-2, 2)
    for index in range(2):
        total = total + passed_along(
            parts[1 + index].astype(jnp.bfloat16), "lat", -offsets[index]
        ).astype(jnp.float32)
    for index in range(2):
        total = total + passed_along(
            parts[3 + index].astype(jnp.bfloat16), "lon", -offsets[index]
        ).astype(jnp.float32)
    return total


def local(queries, key_value, dout):
    tile = key_value[0, 0]
    tokens = tile.shape[0]
    local_heads = queries.shape[3] // HEAD_DIM
    scale = 1.0 / HEAD_DIM**0.5
    near = gather_near(tile)
    key_set = jnp.concatenate([tile[None], near], axis=0).reshape(5 * tokens, 2 * HEAD_DIM)
    keys = key_set[:, :HEAD_DIM]
    values = key_set[:, HEAD_DIM:]
    q_heads = queries[0, 0].reshape(tokens, local_heads, HEAD_DIM).transpose(1, 0, 2)
    d_heads = dout[0, 0].reshape(tokens, local_heads, HEAD_DIM).transpose(1, 0, 2)

    def one_head(carry, operands):
        q_one, d_one = operands
        scores = jnp.dot(q_one, keys.T, preferred_element_type=jnp.float32) * scale
        top = jnp.max(scores, axis=-1, keepdims=True)
        expo = jnp.exp(scores - top)
        probs = expo / jnp.sum(expo, axis=-1, keepdims=True)
        probs_low = probs.astype(jnp.bfloat16)
        dprobs = jnp.dot(d_one, values.T, preferred_element_type=jnp.float32)
        delta = jnp.sum(probs * dprobs, axis=-1, keepdims=True)
        dscore = (probs * (dprobs - delta) * scale).astype(jnp.bfloat16)
        dq_one = jnp.dot(dscore, keys, preferred_element_type=jnp.float32).astype(jnp.bfloat16)
        dkeys = jnp.dot(dscore.T, q_one, preferred_element_type=jnp.float32)
        dvalues = jnp.dot(probs_low.T, d_one, preferred_element_type=jnp.float32)
        return (carry + jnp.concatenate([dkeys, dvalues], axis=1), dq_one)

    start = jnp.zeros((5 * tokens, 2 * HEAD_DIM), jnp.float32)
    grads, dq_heads = lax.scan(one_head, start, (q_heads, d_heads))
    dquery = dq_heads.transpose(1, 0, 2).reshape(tokens, local_heads * HEAD_DIM)[None, None]
    parts = grads.reshape(5, tokens, 2 * HEAD_DIM)
    total = lax.psum_scatter(send_back(parts), "head", scatter_dimension=0, tiled=True)
    return (dquery, total[None, None])


def solution(mesh):
    placed = (
        P("lat", "lon", None, "head"),
        P("lat", "lon", None, None),
        P("lat", "lon", None, "head"),
    )
    return jax.shard_map(
        local,
        mesh=mesh,
        in_specs=placed,
        out_specs=(P("lat", "lon", None, "head"), P("lat", "lon", "head", None)),
        check_vma=False,
    )
```

profile of v0, /device:TPU:1, one launch (start us, length us, event | category | flops | bytes accessed | tf_op | source)
XLA Modules:
  0.0 197.8 jit_solution(14873016717879657640)
XLA Ops:
  7.2 9.5 %collective-permute-start = (bf16[512,128]{1,0:T(8,128)(2,1)}, bf16[512,128]{1,0:T(8,128)(2,1)S(1)}, u32[]{:S(2)}, u32[]{:S(2)}) collective-permute-start(bf16[512,128]{1,0:T(8,128)(2,1)} %bitcast.71), channel_id=1, source_target_pairs={{0,224},{16,240},{32,0},{48,16},{64,32},{80,48},{96,64},{112,80},{... | collective-permute-start | bytes 393224 | tf_op jit(solution)/shard_map/ppermute | solution.py:11
  16.8 2.9 %collective-permute-start.2 = (bf16[512,128]{1,0:T(8,128)(2,1)}, bf16[512,128]{1,0:T(8,128)(2,1)S(1)}, u32[]{:S(2)}, u32[]{:S(2)}) collective-permute-start(bf16[512,128]{1,0:T(8,128)(2,1)} %bitcast.73), channel_id=1, source_target_pairs={{0,12},{2,14},{4,0},{6,2},{8,4},{10,6},{12,8},{14,10},{1,13},{3,15... | collective-permute-start | bytes 393224 | tf_op jit(solution)/shard_map/ppermute | solution.py:11
  24.8 3.5 %collective-permute-done.1 = bf16[512,128]{1,0:T(8,128)(2,1)S(1)} collective-permute-done((bf16[512,128]{1,0:T(8,128)(2,1)}, bf16[512,128]{1,0:T(8,128)(2,1)S(1)}, u32[]{:S(2)}, u32[]{:S(2)}) %collective-permute-start.1) | collective-permute-done | bytes 131104 | tf_op jit(solution)/shard_map/ppermute | solution.py:11
  29.5 132.3 %while.13 = (s32[]{:T(128)}, f32[2560,128]{0,1:T(8,128)}, bf16[8,512,64]{1,2,0:T(8,128)(2,1)}, bf16[8,512,64]{1,2,0:T(8,128)(2,1)}, bf16[2560,64]{1,0:T(8,128)(2...) while((s32[]{:T(128)}, f32[2560,128]{0,1:T(8,128)}, ...), condition=%wide.region_4.5_spmd.clone, body=%wide.region_0.4_spmd.clone.sunk | while | flops 862157312 | bytes 51470948 | solution.py:65
  32.1 2.7 %multiply_reduce_fusion.2 = (f32[512]{0:T(512)S(1)}, f32[512,2560]{1,0:T(8,128)S(1)}) fusion(f32[512]{0:T(512)S(1)} %fusion.54, f32[512,2560]{1,0:T(8,128)S(1)} %get-tuple-element.146, f32[512]{0:T(512)S(1)} %get-tuple-element.147, bf16[2560,64]{1,0:T(8,128)(2,1)} %get-tuple-element.174, bf16[8,512,64]{1,2,0:T(8,128)(2,1)} %get-tuple-element.173, ...), kind=kOutput, calls=%fused_computation.1.clone.1 | convolution fusion | flops 173014528 | bytes 11213312 | tf_op jit(solution)/shard_map/while/body/eval_jaxpr/dot_general | solution.py:56
  36.6 2.3 %fusion.56 = f32[2560,64]{0,1:T(8,128)} fusion(bf16[512,2560]{1,0:T(8,128)(2,1)S(1)} %multiply_convert_fusion.2, bf16[8,512,64]{1,2,0:T(8,128)(2,1)} %get-tuple-element.171, s32[]{:T(128)} %get-tuple-element.159), kind=kOutput, calls=%fused_computation.15.clone.1 | convolution fusion | flops 167772160 | bytes 3342848 | tf_op jit(solution)/shard_map/while/body/eval_jaxpr/dot_general | solution.py:60
  38.8 2.8 %fusion.55 = f32[2560,64]{0,1:T(8,128)} fusion(bf16[8,512,64]{1,2,0:T(8,128)(2,1)} %get-tuple-element.173, s32[]{:T(128)} %get-tuple-element.159, f32[512,2560]{1,0:T(8,128)S(1)} %get-tuple-element.146, f32[512]{0:T(512)S(1)} %fusion.54, f32[512]{0:T(512)S(1)} %get-tuple-element.147), kind=kOutput, calls=%fused_computation.6.clone.1 | convolution fusion | flops 171704320 | bytes 5968384 | tf_op jit(solution)/shard_map/while/body/eval_jaxpr/dot_general | solution.py:61
  41.6 2.5 %maximum_add_fusion.2 = f32[2560,128]{0,1:T(8,128)} fusion(f32[2560,64]{0,1:T(8,128)} %fusion.55, f32[2560,64]{0,1:T(8,128)} %fusion.56, f32[2560,128]{0,1:T(8,128)} %get-tuple-element.160, pred[]{:T(512)S(6)} %compare.3), kind=kLoop, calls=%fused_computation.8.clone.1 | loop fusion | flops 983040 | bytes 3932161 | tf_op jit(solution)/shard_map/while/body/eval_jaxpr/add | solution.py:62
  48.3 2.7 %multiply_reduce_fusion.2 = (f32[512]{0:T(512)S(1)}, f32[512,2560]{1,0:T(8,128)S(1)}) fusion(f32[512]{0:T(512)S(1)} %fusion.54, f32[512,2560]{1,0:T(8,128)S(1)} %get-tuple-element.146, f32[512]{0:T(512)S(1)} %get-tuple-element.147, bf16[2560,64]{1,0:T(8,128)(2,1)} %get-tuple-element.174, bf16[8,512,64]{1,2,0:T(8,128)(2,1)} %get-tuple-element.173, ...), kind=kOutput, calls=%fused_computation.1.clone.1 | convolution fusion | flops 173014528 | bytes 11213312 | tf_op jit(solution)/shard_map/while/body/eval_jaxpr/dot_general | solution.py:56
  55.0 2.8 %fusion.55 = f32[2560,64]{0,1:T(8,128)} fusion(bf16[8,512,64]{1,2,0:T(8,128)(2,1)} %get-tuple-element.173, s32[]{:T(128)} %get-tuple-element.159, f32[512,2560]{1,0:T(8,128)S(1)} %get-tuple-element.146, f32[512]{0:T(512)S(1)} %fusion.54, f32[512]{0:T(512)S(1)} %get-tuple-element.147), kind=kOutput, calls=%fused_computation.6.clone.1 | convolution fusion | flops 171704320 | bytes 5968384 | tf_op jit(solution)/shard_map/while/body/eval_jaxpr/dot_general | solution.py:61
  57.8 2.9 %maximum_add_fusion.2 = f32[2560,128]{0,1:T(8,128)} fusion(f32[2560,64]{0,1:T(8,128)} %fusion.55, f32[2560,64]{0,1:T(8,128)} %fusion.56, f32[2560,128]{0,1:T(8,128)} %get-tuple-element.160, pred[]{:T(512)S(6)} %compare.3), kind=kLoop, calls=%fused_computation.8.clone.1 | loop fusion | flops 983040 | bytes 3932161 | tf_op jit(solution)/shard_map/while/body/eval_jaxpr/add | solution.py:62
  64.9 2.7 %multiply_reduce_fusion.2 = (f32[512]{0:T(512)S(1)}, f32[512,2560]{1,0:T(8,128)S(1)}) fusion(f32[512]{0:T(512)S(1)} %fusion.54, f32[512,2560]{1,0:T(8,128)S(1)} %get-tuple-element.146, f32[512]{0:T(512)S(1)} %get-tuple-element.147, bf16[2560,64]{1,0:T(8,128)(2,1)} %get-tuple-element.174, bf16[8,512,64]{1,2,0:T(8,128)(2,1)} %get-tuple-element.173, ...), kind=kOutput, calls=%fused_computation.1.clone.1 | convolution fusion | flops 173014528 | bytes 11213312 | tf_op jit(solution)/shard_map/while/body/eval_jaxpr/dot_general | solution.py:56
  71.6 2.8 %fusion.55 = f32[2560,64]{0,1:T(8,128)} fusion(bf16[8,512,64]{1,2,0:T(8,128)(2,1)} %get-tuple-element.173, s32[]{:T(128)} %get-tuple-element.159, f32[512,2560]{1,0:T(8,128)S(1)} %get-tuple-element.146, f32[512]{0:T(512)S(1)} %fusion.54, f32[512]{0:T(512)S(1)} %get-tuple-element.147), kind=kOutput, calls=%fused_computation.6.clone.1 | convolution fusion | flops 171704320 | bytes 5968384 | tf_op jit(solution)/shard_map/while/body/eval_jaxpr/dot_general | solution.py:61
  74.4 2.9 %maximum_add_fusion.2 = f32[2560,128]{0,1:T(8,128)} fusion(f32[2560,64]{0,1:T(8,128)} %fusion.55, f32[2560,64]{0,1:T(8,128)} %fusion.56, f32[2560,128]{0,1:T(8,128)} %get-tuple-element.160, pred[]{:T(512)S(6)} %compare.3), kind=kLoop, calls=%fused_computation.8.clone.1 | loop fusion | flops 983040 | bytes 3932161 | tf_op jit(solution)/shard_map/while/body/eval_jaxpr/add | solution.py:62
  81.5 2.7 %multiply_reduce_fusion.2 = (f32[512]{0:T(512)S(1)}, f32[512,2560]{1,0:T(8,128)S(1)}) fusion(f32[512]{0:T(512)S(1)} %fusion.54, f32[512,2560]{1,0:T(8,128)S(1)} %get-tuple-element.146, f32[512]{0:T(512)S(1)} %get-tuple-element.147, bf16[2560,64]{1,0:T(8,128)(2,1)} %get-tuple-element.174, bf16[8,512,64]{1,2,0:T(8,128)(2,1)} %get-tuple-element.173, ...), kind=kOutput, calls=%fused_computation.1.clone.1 | convolution fusion | flops 173014528 | bytes 11213312 | tf_op jit(solution)/shard_map/while/body/eval_jaxpr/dot_general | solution.py:56
  88.2 2.8 %fusion.55 = f32[2560,64]{0,1:T(8,128)} fusion(bf16[8,512,64]{1,2,0:T(8,128)(2,1)} %get-tuple-element.173, s32[]{:T(128)} %get-tuple-element.159, f32[512,2560]{1,0:T(8,128)S(1)} %get-tuple-element.146, f32[512]{0:T(512)S(1)} %fusion.54, f32[512]{0:T(512)S(1)} %get-tuple-element.147), kind=kOutput, calls=%fused_computation.6.clone.1 | convolution fusion | flops 171704320 | bytes 5968384 | tf_op jit(solution)/shard_map/while/body/eval_jaxpr/dot_general | solution.py:61
  91.0 2.9 %maximum_add_fusion.2 = f32[2560,128]{0,1:T(8,128)} fusion(f32[2560,64]{0,1:T(8,128)} %fusion.55, f32[2560,64]{0,1:T(8,128)} %fusion.56, f32[2560,128]{0,1:T(8,128)} %get-tuple-element.160, pred[]{:T(512)S(6)} %compare.3), kind=kLoop, calls=%fused_computation.8.clone.1 | loop fusion | flops 983040 | bytes 3932161 | tf_op jit(solution)/shard_map/while/body/eval_jaxpr/add | solution.py:62
  98.1 2.7 %multiply_reduce_fusion.2 = (f32[512]{0:T(512)S(1)}, f32[512,2560]{1,0:T(8,128)S(1)}) fusion(f32[512]{0:T(512)S(1)} %fusion.54, f32[512,2560]{1,0:T(8,128)S(1)} %get-tuple-element.146, f32[512]{0:T(512)S(1)} %get-tuple-element.147, bf16[2560,64]{1,0:T(8,128)(2,1)} %get-tuple-element.174, bf16[8,512,64]{1,2,0:T(8,128)(2,1)} %get-tuple-element.173, ...), kind=kOutput, calls=%fused_computation.1.clone.1 | convolution fusion | flops 173014528 | bytes 11213312 | tf_op jit(solution)/shard_map/while/body/eval_jaxpr/dot_general | solution.py:56
  104.8 2.8 %fusion.55 = f32[2560,64]{0,1:T(8,128)} fusion(bf16[8,512,64]{1,2,0:T(8,128)(2,1)} %get-tuple-element.173, s32[]{:T(128)} %get-tuple-element.159, f32[512,2560]{1,0:T(8,128)S(1)} %get-tuple-element.146, f32[512]{0:T(512)S(1)} %fusion.54, f32[512]{0:T(512)S(1)} %get-tuple-element.147), kind=kOutput, calls=%fused_computation.6.clone.1 | convolution fusion | flops 171704320 | bytes 5968384 | tf_op jit(solution)/shard_map/while/body/eval_jaxpr/dot_general | solution.py:61
  107.5 2.9 %maximum_add_fusion.2 = f32[2560,128]{0,1:T(8,128)} fusion(f32[2560,64]{0,1:T(8,128)} %fusion.55, f32[2560,64]{0,1:T(8,128)} %fusion.56, f32[2560,128]{0,1:T(8,128)} %get-tuple-element.160, pred[]{:T(512)S(6)} %compare.3), kind=kLoop, calls=%fused_computation.8.clone.1 | loop fusion | flops 983040 | bytes 3932161 | tf_op jit(solution)/shard_map/while/body/eval_jaxpr/add | solution.py:62
  114.7 2.7 %multiply_reduce_fusion.2 = (f32[512]{0:T(512)S(1)}, f32[512,2560]{1,0:T(8,128)S(1)}) fusion(f32[512]{0:T(512)S(1)} %fusion.54, f32[512,2560]{1,0:T(8,128)S(1)} %get-tuple-element.146, f32[512]{0:T(512)S(1)} %get-tuple-element.147, bf16[2560,64]{1,0:T(8,128)(2,1)} %get-tuple-element.174, bf16[8,512,64]{1,2,0:T(8,128)(2,1)} %get-tuple-element.173, ...), kind=kOutput, calls=%fused_computation.1.clone.1 | convolution fusion | flops 173014528 | bytes 11213312 | tf_op jit(solution)/shard_map/while/body/eval_jaxpr/dot_general | solution.py:56
  121.4 2.8 %fusion.55 = f32[2560,64]{0,1:T(8,128)} fusion(bf16[8,512,64]{1,2,0:T(8,128)(2,1)} %get-tuple-element.173, s32[]{:T(128)} %get-tuple-element.159, f32[512,2560]{1,0:T(8,128)S(1)} %get-tuple-element.146, f32[512]{0:T(512)S(1)} %fusion.54, f32[512]{0:T(512)S(1)} %get-tuple-element.147), kind=kOutput, calls=%fused_computation.6.clone.1 | convolution fusion | flops 171704320 | bytes 5968384 | tf_op jit(solution)/shard_map/while/body/eval_jaxpr/dot_general | solution.py:61
  124.1 2.9 %maximum_add_fusion.2 = f32[2560,128]{0,1:T(8,128)} fusion(f32[2560,64]{0,1:T(8,128)} %fusion.55, f32[2560,64]{0,1:T(8,128)} %fusion.56, f32[2560,128]{0,1:T(8,128)} %get-tuple-element.160, pred[]{:T(512)S(6)} %compare.3), kind=kLoop, calls=%fused_computation.8.clone.1 | loop fusion | flops 983040 | bytes 3932161 | tf_op jit(solution)/shard_map/while/body/eval_jaxpr/add | solution.py:62
  131.2 2.7 %multiply_reduce_fusion.2 = (f32[512]{0:T(512)S(1)}, f32[512,2560]{1,0:T(8,128)S(1)}) fusion(f32[512]{0:T(512)S(1)} %fusion.54, f32[512,2560]{1,0:T(8,128)S(1)} %get-tuple-element.146, f32[512]{0:T(512)S(1)} %get-tuple-element.147, bf16[2560,64]{1,0:T(8,128)(2,1)} %get-tuple-element.174, bf16[8,512,64]{1,2,0:T(8,128)(2,1)} %get-tuple-element.173, ...), kind=kOutput, calls=%fused_computation.1.clone.1 | convolution fusion | flops 173014528 | bytes 11213312 | tf_op jit(solution)/shard_map/while/body/eval_jaxpr/dot_general | solution.py:56
  138.0 2.8 %fusion.55 = f32[2560,64]{0,1:T(8,128)} fusion(bf16[8,512,64]{1,2,0:T(8,128)(2,1)} %get-tuple-element.173, s32[]{:T(128)} %get-tuple-element.159, f32[512,2560]{1,0:T(8,128)S(1)} %get-tuple-element.146, f32[512]{0:T(512)S(1)} %fusion.54, f32[512]{0:T(512)S(1)} %get-tuple-element.147), kind=kOutput, calls=%fused_computation.6.clone.1 | convolution fusion | flops 171704320 | bytes 5968384 | tf_op jit(solution)/shard_map/while/body/eval_jaxpr/dot_general | solution.py:61
  140.7 2.9 %maximum_add_fusion.2 = f32[2560,128]{0,1:T(8,128)} fusion(f32[2560,64]{0,1:T(8,128)} %fusion.55, f32[2560,64]{0,1:T(8,128)} %fusion.56, f32[2560,128]{0,1:T(8,128)} %get-tuple-element.160, pred[]{:T(512)S(6)} %compare.3), kind=kLoop, calls=%fused_computation.8.clone.1 | loop fusion | flops 983040 | bytes 3932161 | tf_op jit(solution)/shard_map/while/body/eval_jaxpr/add | solution.py:62
  147.8 2.7 %multiply_reduce_fusion.2 = (f32[512]{0:T(512)S(1)}, f32[512,2560]{1,0:T(8,128)S(1)}) fusion(f32[512]{0:T(512)S(1)} %fusion.54, f32[512,2560]{1,0:T(8,128)S(1)} %get-tuple-element.146, f32[512]{0:T(512)S(1)} %get-tuple-element.147, bf16[2560,64]{1,0:T(8,128)(2,1)} %get-tuple-element.174, bf16[8,512,64]{1,2,0:T(8,128)(2,1)} %get-tuple-element.173, ...), kind=kOutput, calls=%fused_computation.1.clone.1 | convolution fusion | flops 173014528 | bytes 11213312 | tf_op jit(solution)/shard_map/while/body/eval_jaxpr/dot_general | solution.py:56
  154.5 2.8 %fusion.55 = f32[2560,64]{0,1:T(8,128)} fusion(bf16[8,512,64]{1,2,0:T(8,128)(2,1)} %get-tuple-element.173, s32[]{:T(128)} %get-tuple-element.159, f32[512,2560]{1,0:T(8,128)S(1)} %get-tuple-element.146, f32[512]{0:T(512)S(1)} %fusion.54, f32[512]{0:T(512)S(1)} %get-tuple-element.147), kind=kOutput, calls=%fused_computation.6.clone.1 | convolution fusion | flops 171704320 | bytes 5968384 | tf_op jit(solution)/shard_map/while/body/eval_jaxpr/dot_general | solution.py:61
  157.3 2.9 %maximum_add_fusion.2 = f32[2560,128]{0,1:T(8,128)} fusion(f32[2560,64]{0,1:T(8,128)} %fusion.55, f32[2560,64]{0,1:T(8,128)} %fusion.56, f32[2560,128]{0,1:T(8,128)} %get-tuple-element.160, pred[]{:T(512)S(6)} %compare.3), kind=kLoop, calls=%fused_computation.8.clone.1 | loop fusion | flops 983040 | bytes 3932161 | tf_op jit(solution)/shard_map/while/body/eval_jaxpr/add | solution.py:62
  163.8 6.0 %collective-permute-start.5 = (bf16[512,128]{1,0:T(8,128)(2,1)S(1)}, bf16[512,128]{1,0:T(8,128)(2,1)S(1)}, u32[]{:S(2)}, u32[]{:S(2)}) collective-permute-start(bf16[512,128]{1,0:T(8,128)(2,1)S(1)} %get-tuple-element.96), channel_id=1, source_target_pairs={{0,224},{16,240},{32,0},{48,16},{64,32},{80,48},{96,64},{112,80},{... | collective-permute-start | bytes 393224 | tf_op jit(solution)/shard_map/ppermute | solution.py:11
  173.8 2.5 %collective-permute-done.6 = bf16[512,128]{1,0:T(8,128)(2,1)S(1)} collective-permute-done((bf16[512,128]{1,0:T(8,128)(2,1)S(1)}, bf16[512,128]{1,0:T(8,128)(2,1)S(1)}, u32[]{:S(2)}, u32[]{:S(2)}) %collective-permute-start.6) | collective-permute-done | bytes 131104 | tf_op jit(solution)/shard_map/ppermute | solution.py:11
  178.8 12.2 %reduce-scatter.2.cloned.1.call-done = f32[256,128]{1,0:T(8,128)} async-done(((f32[512,128]{1,0:T(8,128)}), f32[256,128]{1,0:T(8,128)}) %reduce-scatter.2.cloned.1.call-update) | async-done | bytes 131088 | tf_op jit(solution)/shard_map/reduce_scatter | solution.py:68
  (69 shorter events, 78.0 us)
Async XLA Ops:
  7.2 183.8 %reduce-scatter.2.cloned.1.call-start = ((), (), s32[]{:S(2)}) async-start(), calls=%async_computation.1 | async-start | bytes 393216 | tf_op jit(solution)/shard_map/reduce_scatter | solution.py:68
  7.2 17.5 %collective-permute-start = (bf16[512,128]{1,0:T(8,128)(2,1)}, bf16[512,128]{1,0:T(8,128)(2,1)S(1)}, u32[]{:S(2)}, u32[]{:S(2)}) collective-permute-start(bf16[512,128]{1,0:T(8,128)(2,1)} %bitcast.71), channel_id=1, source_target_pairs={{0,224},{16,240},{32,0},{48,16},{64,32},{80,48},{96,64},{112,80},{... | collective-permute-start | bytes 393224 | tf_op jit(solution)/shard_map/ppermute | solution.py:11
  16.8 11.5 %collective-permute-start.1 = (bf16[512,128]{1,0:T(8,128)(2,1)}, bf16[512,128]{1,0:T(8,128)(2,1)S(1)}, u32[]{:S(2)}, u32[]{:S(2)}) collective-permute-start(bf16[512,128]{1,0:T(8,128)(2,1)} %bitcast.72), channel_id=1, source_target_pairs={{0,32},{16,48},{32,64},{48,80},{64,96},{80,112},{96,128},{112,144}... | collective-permute-start | bytes 393224 | tf_op jit(solution)/shard_map/ppermute | solution.py:11
  16.8 11.5 %collective-permute-start.2 = (bf16[512,128]{1,0:T(8,128)(2,1)}, bf16[512,128]{1,0:T(8,128)(2,1)S(1)}, u32[]{:S(2)}, u32[]{:S(2)}) collective-permute-start(bf16[512,128]{1,0:T(8,128)(2,1)} %bitcast.73), channel_id=1, source_target_pairs={{0,12},{2,14},{4,0},{6,2},{8,4},{10,6},{12,8},{14,10},{1,13},{3,15... | collective-permute-start | bytes 393224 | tf_op jit(solution)/shard_map/ppermute | solution.py:11
  19.6 8.7 %collective-permute-start.3 = (bf16[512,128]{1,0:T(8,128)(2,1)}, bf16[512,128]{1,0:T(8,128)(2,1)S(1)}, u32[]{:S(2)}, u32[]{:S(2)}) collective-permute-start(bf16[512,128]{1,0:T(8,128)(2,1)} %bitcast.74), channel_id=1, source_target_pairs={{0,4},{2,6},{4,8},{6,10},{8,12},{10,14},{12,0},{14,2},{1,5},{3,7},... | collective-permute-start | bytes 393224 | tf_op jit(solution)/shard_map/ppermute | solution.py:11
  161.8 16.0 %copy-start = (bf16[8,512,64]{1,2,0:T(8,128)(2,1)S(1)}, bf16[8,512,64]{1,2,0:T(8,128)(2,1)}, u32[]{:S(2)}) copy-start(bf16[8,512,64]{1,2,0:T(8,128)(2,1)} %get-tuple-element.40) | copy-start | bytes 1572868
  163.7 10.1 %collective-permute-start.4 = (bf16[512,128]{1,0:T(8,128)(2,1)S(1)}, bf16[512,128]{1,0:T(8,128)(2,1)S(1)}, u32[]{:S(2)}, u32[]{:S(2)}) collective-permute-start(bf16[512,128]{1,0:T(8,128)(2,1)S(1)} %get-tuple-element.93), channel_id=1, source_target_pairs={{0,32},{16,48},{32,64},{48,80},{64,96},{80,112},{96,128},{112,144}... | collective-permute-start | bytes 393224 | tf_op jit(solution)/shard_map/ppermute | solution.py:11
  163.8 10.0 %collective-permute-start.5 = (bf16[512,128]{1,0:T(8,128)(2,1)S(1)}, bf16[512,128]{1,0:T(8,128)(2,1)S(1)}, u32[]{:S(2)}, u32[]{:S(2)}) collective-permute-start(bf16[512,128]{1,0:T(8,128)(2,1)S(1)} %get-tuple-element.96), channel_id=1, source_target_pairs={{0,224},{16,240},{32,0},{48,16},{64,32},{80,48},{96,64},{112,80},{... | collective-permute-start | bytes 393224 | tf_op jit(solution)/shard_map/ppermute | solution.py:11
  169.7 6.5 %collective-permute-start.6 = (bf16[512,128]{1,0:T(8,128)(2,1)S(1)}, bf16[512,128]{1,0:T(8,128)(2,1)S(1)}, u32[]{:S(2)}, u32[]{:S(2)}) collective-permute-start(bf16[512,128]{1,0:T(8,128)(2,1)S(1)} %get-tuple-element.95), channel_id=1, source_target_pairs={{0,4},{2,6},{4,8},{6,10},{8,12},{10,14},{12,0},{14,2},{1,5},{3,7},... | collective-permute-start | bytes 393224 | tf_op jit(solution)/shard_map/ppermute | solution.py:11
  171.6 5.3 %collective-permute-start.7 = (bf16[512,128]{1,0:T(8,128)(2,1)S(1)}, bf16[512,128]{1,0:T(8,128)(2,1)S(1)}, u32[]{:S(2)}, u32[]{:S(2)}) collective-permute-start(bf16[512,128]{1,0:T(8,128)(2,1)S(1)} %get-tuple-element.94), channel_id=1, source_target_pairs={{0,12},{2,14},{4,0},{6,2},{8,4},{10,6},{12,8},{14,10},{1,13},{3,15... | collective-permute-start | bytes 393224 | tf_op jit(solution)/shard_map/ppermute | solution.py:11
Sparse Core Ops, SparseCore 0:
  177.9 13.0 reduce-scatter.1
where the time goes:
time: 200 us; the launch traced here: 198 us
  matrix products  88.7 us (44%)
  other arithmetic  44.3 us (22%)
  starting transfers between devices  22.5 us (11%)
  waiting for transfers between devices  19 us (10%)
  between operations  14.1 us (7%)
  local copies, waits for them, and re-layouts  9.03 us (5%)
    add x8, other arithmetic, one_head(): return (carry + jnp.concatenate([dkeys, dvalues], axis=1), dq_one)  23 us
    ppermute x8, starting transfers between devices, passed_along(): lax.ppermute(array, axis, [(i, (i + by) % peers) for i in range(peers)])  22.4 us
    dot_general x8, matrix products, one_head(): dvalues = jnp.dot(probs_low.T, d_one, preferred_element_type=jnp.float32)  22.1 us
    dot_general x8, matrix products, one_head(): dprobs = jnp.dot(d_one, values.T, preferred_element_type=jnp.float32)  21.8 us
    dot_general x8, matrix products, one_head(): dkeys = jnp.dot(dscore.T, q_one, preferred_element_type=jnp.float32)  18.1 us
    dot_general x8, matrix products, one_head(): scores = jnp.dot(q_one, keys.T, preferred_element_type=jnp.float32) * scale  14.4 us
    convert_element_type x8, other arithmetic, one_head(): dscore = (probs * (dprobs - delta) * scale).astype(jnp.bfloat16)  13.8 us
    dot_general x8, matrix products, one_head(): jnp.dot(dscore, keys, preferred_element_type=jnp.float32)  12.4 us
  transfers between devices with their start and end apart: 9, of which 5 were waited for; matrix products, arithmetic and copies ran while one was open for 3% of the time, Pallas kernels for 0%

commit v1 on v0

v1 whole, which is shorter than its diff:
```python
import functools

import jax
import jax.numpy as jnp
from jax import lax
from jax.experimental import pallas as pl
from jax.experimental.pallas import tpu as pltpu
from jax.sharding import PartitionSpec as P
HD=64
CH=256
def kernel(heads, tok, tiles, q_ref, d_ref, *rest):
    kv_refs=rest[:tiles]; dq_ref, g_ref = rest[tiles:tiles+2]
    qz, dz, kT, s_ref, dp_ref, e_ref, acc, dqt, w_ref, stat = rest[tiles+2:]
    per=tok//CH; nch=tiles*per
    scale=1.0/HD**0.5
    c2=1.4426950408889634*scale
    f32=jnp.float32; bf=jnp.bfloat16
    def kvc(c): return kv_refs[c//per][(c%per)*CH:(c%per+1)*CH,:]
    zero=jnp.zeros((HD,tok),bf)
    qT=q_ref[...].T; dT=d_ref[...].T
    for h in range(heads):
        qz[h,:HD,:]=qT[h*HD:(h+1)*HD,:]; qz[h,HD:,:]=zero
        dz[h,HD:,:]=dT[h*HD:(h+1)*HD,:]; dz[h,:HD,:]=zero
    for c in range(nch):
        kT[:,c*CH:(c+1)*CH]=kvc(c).T[:HD,:]
        acc[c]=jnp.zeros((CH,2*HD),f32)
    def g8(x): return x.reshape(CH//8,8,tok)
    def allmax(x):
        return jnp.broadcast_to(jnp.max(x,axis=0,keepdims=True),x.shape)
    def allsum(x):
        return jnp.broadcast_to(jnp.sum(x,axis=0,keepdims=True),x.shape)
    NEG=jnp.full((8,tok),-jnp.inf,f32); Z8=jnp.zeros((8,tok),f32)
    def step(i, do1, do2, do3):
        mx=NEG; l8=Z8; D8=Z8
        if do2: m8=stat[0]
        if do3:
            delta8=stat[1]
            dqa=jnp.zeros((HD,tok),f32)
        for c in range(nch):
            if do3:
                e=e_ref[c]
                t=(g8(dp_ref[c])-delta8[None]).astype(bf).reshape(CH,tok)
                g=e*t
                r=jnp.dot(jnp.concatenate([g,e],axis=1),w_ref[...],preferred_element_type=f32)
                acc[c]+=r
                dqa=dqa+jnp.dot(kT[:,c*CH:(c+1)*CH],g,preferred_element_type=f32)
            if do2:
                dp=jnp.dot(kvc(c),dz[i],preferred_element_type=f32)
                e=jnp.exp2((g8(s_ref[c])-m8[None])*c2)
                l8=l8+jnp.sum(e,axis=0)
                D8=D8+jnp.sum(e*g8(dp),axis=0)
                e_ref[c]=e.reshape(CH,tok).astype(bf)
                dp_ref[c]=dp
            if do1:
                s=jnp.dot(kvc(c),qz[i+1],preferred_element_type=f32)
                s_ref[c]=s
                mx=jnp.maximum(mx,jnp.max(g8(s),axis=0))
        if do3:
            dqt[i-1]=(dqa*(stat[2,:1]*scale)).astype(bf)
        if do1: stat[0]=allmax(mx)
        if do2:
            l=allsum(l8); r=1.0/l
            stat[1]=allsum(D8)*r
            stat[2]=r
            wt=jnp.concatenate([(qz[i].astype(f32)*(r[:1]*scale)).astype(bf),(dz[i].astype(f32)*r[:1]).astype(bf)],axis=1)
            w_ref[...]=wt.T
    step(-1,True,False,False)
    step(0,True,True,False)
    def body(i,carry):
        step(i,True,True,True); return carry
    lax.fori_loop(1,heads-1,body,0)
    step(heads-1,False,True,True)
    step(heads,False,False,True)
    dq_ref[...]=dqt[...].reshape(heads*HD,tok).T
    for c in range(nch):
        g_ref[c*CH:(c+1)*CH,:]=acc[c]
def attn_grads(q,d,kvs):
    tok,w=q.shape; heads=w//HD; tiles=len(kvs); nch=tiles*tok//CH
    f32=jnp.float32; bf=jnp.bfloat16
    V=pl.BlockSpec(memory_space=pltpu.VMEM)
    return pl.pallas_call(functools.partial(kernel,heads,tok,tiles),
        out_shape=(jax.ShapeDtypeStruct((tok,w),bf),jax.ShapeDtypeStruct((tiles*tok,2*HD),f32)),
        in_specs=[V]*(2+tiles),out_specs=(V,V),
        scratch_shapes=[pltpu.VMEM((heads,2*HD,tok),bf),pltpu.VMEM((heads,2*HD,tok),bf),pltpu.VMEM((HD,tiles*tok),bf),
          pltpu.VMEM((nch,CH,tok),f32),pltpu.VMEM((nch,CH,tok),f32),pltpu.VMEM((nch,CH,tok),bf),
          pltpu.VMEM((nch,CH,2*HD),f32),pltpu.VMEM((heads,HD,tok),bf),pltpu.VMEM((2*tok,2*HD),bf),pltpu.VMEM((3,8,tok),f32)],
        compiler_params=pltpu.CompilerParams(vmem_limit_bytes=60*2**20),name="attn_grads")(q,d,*kvs)


def shifted(array, axis, by):
    peers = lax.axis_size(axis)
    return lax.ppermute(array, axis, [(i, (i + by) % peers) for i in range(peers)])


STEPS = (("lat", -2), ("lat", 2), ("lon", -2), ("lon", 2))


def local(queries, key_value, dout):
    tile = key_value[0, 0]
    tok = tile.shape[0]
    near = [shifted(tile, axis, by) for axis, by in STEPS]
    dquery, grads = attn_grads(queries[0, 0], dout[0, 0], [tile] + near)
    halves = grads.reshape(5, 2, tok // 2, 2 * HD)
    me = lax.axis_index("head")
    keep = lax.dynamic_index_in_dim(halves, me, 1, keepdims=False)
    send = lax.dynamic_index_in_dim(halves, 1 - me, 1, keepdims=False)
    both = keep + shifted(send, "head", 1)
    total = both[0]
    for index, (axis, by) in enumerate(STEPS):
        back = shifted(both[1 + index].astype(jnp.bfloat16), axis, -by)
        total = total + back.astype(jnp.float32)
    return dquery[None, None], total[None, None]


def solution(mesh):
    placed = (
        P("lat", "lon", None, "head"),
        P("lat", "lon", None, None),
        P("lat", "lon", None, "head"),
    )
    return jax.shard_map(
        local,
        mesh=mesh,
        in_specs=placed,
        out_specs=(P("lat", "lon", None, "head"), P("lat", "lon", "head", None)),
        check_vma=False,
    )
```

time: 200 us -> 70.1 us (0.35)
  matrix products: 88.7 us -> 0 us
  other arithmetic: 44.3 us -> 0.8 us
  Pallas kernels: 0 us -> 32.6 us
  between operations: 14.1 us -> 0.68 us
  waiting for transfers between devices: 19 us -> 8.13 us
  local copies, waits for them, and re-layouts: 9.03 us -> 1.91 us
  starting transfers between devices: 22.5 us -> 25.2 us
    dot_general x40 -> x0, matrix products: 88.7 us -> none  [the longest x8 22.1 us: one_head(): dvalues = jnp.dot(probs_low.T, d_one, preferred_element_type=jnp.float32)]
    pallas_call x0 -> x1, Pallas kernels: none -> 32.6 us  [attn_grads(): pl.pallas_call(functools.partial(kernel, heads, tok, tiles), out_shape=(j...]
    add x9 -> x0, other arithmetic: 23.8 us -> none  [the longest x8 23 us: one_head(): return (carry + jnp.concatenate([dkeys, dvalues], axis=1), dq_one)]
    convert_element_type x8 -> x0, other arithmetic: 13.8 us -> none  [one_head(): dscore = (probs * (dprobs - delta) * scale).astype(jnp.bfloat16)]
    reduce_scatter x1 -> x0, waiting for transfers between devices: 12.2 us -> none  [local(): lax.psum_scatter(send_back(parts), 'head', scatter_dimension=0, tiled=True)]
    reduce_sum x8 -> x0, other arithmetic: 6.75 us -> none  [one_head(): probs = expo / jnp.sum(expo, axis=-1, keepdims=True)]
    unnamed x9 -> x10, local copies, waits for them, and re-layouts: 6.08 us -> 0.66 us
    ppermute x8 -> x9, starting transfers between devices: 22.4 us -> 25.2 us  [shifted(): lax.ppermute(array, axis, [(i, (i + by) % peers) for i in range(peers)])]
  transfers between devices with their start and end apart: 9 -> 9, of which waited for: 5 -> 4; matrix products, arithmetic and copies ran while one was open for 3% -> 0% of each run, Pallas kernels for 0% -> 0%
where the time goes in v1:
time: 70.1 us; the launch traced here: 69.4 us
  Pallas kernels  32.6 us (47%)
  starting transfers between devices  25.2 us (36%)
  waiting for transfers between devices  8.13 us (12%)
  local copies, waits for them, and re-layouts  1.91 us (3%)
  other arithmetic  0.8 us (1%)
    pallas_call x1, Pallas kernels, attn_grads(): pl.pallas_call(functools.partial(kernel, heads, tok, tiles), out_shape=(j...  32.6 us
    ppermute x9, starting transfers between devices, shifted(): lax.ppermute(array, axis, [(i, (i + by) % peers) for i in range(peers)])  25.2 us
    ppermute x9, waiting for transfers between devices, shifted(): lax.ppermute(array, axis, [(i, (i + by) % peers) for i in range(peers)])  8.13 us
  transfers between devices with their start and end apart: 9, of which 4 were waited for; matrix products, arithmetic and copies ran while one was open for 0% of the time, Pallas kernels for 0%

profile of v1, /device:TPU:1, one launch (start us, length us, event | category | flops | bytes accessed | tf_op | source)
XLA Modules:
  0.0 69.4 jit_solution(5243388569481262534)
XLA Ops:
  0.6 3.6 %collective-permute-start.3 = (bf16[512,128]{1,0:T(8,128)(2,1)}, bf16[512,128]{1,0:T(8,128)(2,1)S(1)}, u32[]{:S(2)}, u32[]{:S(2)}) collective-permute-start(bf16[512,128]{1,0:T(8,128)(2,1)} %bitcast.36), channel_id=1, source_target_pairs={{0,4},{2,6},{4,8},{6,10},{8,12},{10,14},{12,0},{14,2},{1,5},{3,7},... | collective-permute-start | bytes 393224 | tf_op jit(solution)/shard_map/ppermute | solution.py:92
  4.3 1.1 %collective-permute-start.2 = (bf16[512,128]{1,0:T(8,128)(2,1)}, bf16[512,128]{1,0:T(8,128)(2,1)S(1)}, u32[]{:S(2)}, u32[]{:S(2)}) collective-permute-start(bf16[512,128]{1,0:T(8,128)(2,1)} %bitcast.37), channel_id=1, source_target_pairs={{0,12},{2,14},{4,0},{6,2},{8,4},{10,6},{12,8},{14,10},{1,13},{3,15... | collective-permute-start | bytes 393224 | tf_op jit(solution)/shard_map/ppermute | solution.py:92
  5.4 3.0 %collective-permute-start.1 = (bf16[512,128]{1,0:T(8,128)(2,1)}, bf16[512,128]{1,0:T(8,128)(2,1)S(1)}, u32[]{:S(2)}, u32[]{:S(2)}) collective-permute-start(bf16[512,128]{1,0:T(8,128)(2,1)} %bitcast.38), channel_id=1, source_target_pairs={{0,32},{16,48},{32,64},{48,80},{64,96},{80,112},{96,128},{112,144}... | collective-permute-start | bytes 393224 | tf_op jit(solution)/shard_map/ppermute | solution.py:92
  8.4 5.7 %collective-permute-start = (bf16[512,128]{1,0:T(8,128)(2,1)}, bf16[512,128]{1,0:T(8,128)(2,1)S(1)}, u32[]{:S(2)}, u32[]{:S(2)}) collective-permute-start(bf16[512,128]{1,0:T(8,128)(2,1)} %bitcast.39), channel_id=1, source_target_pairs={{0,224},{16,240},{32,0},{48,16},{64,32},{80,48},{96,64},{112,80},{... | collective-permute-start | bytes 393224 | tf_op jit(solution)/shard_map/ppermute | solution.py:92
  14.0 0.0 collective-permute-done.3.rest_4_
  14.1 0.0 copy-start.1
  14.1 0.0 collective-permute-done.2.rest_3_
  14.1 0.0 copy-start.2
  14.1 2.9 %collective-permute-done.1.rest_2_ = bf16[512,128]{1,0:T(8,128)(2,1)S(1)} collective-permute-done((bf16[512,128]{1,0:T(8,128)(2,1)}, bf16[512,128]{1,0:T(8,128)(2,1)S(1)}, u32[]{:S(2)}, u32[]{:S(2)}) %collective-permute-start.1) | collective-permute-done | bytes 131104 | tf_op jit(solution)/shard_map/ppermute | solution.py:92
  17.0 0.0 copy-start.3
  17.0 2.1 %collective-permute-done.rest_1_ = bf16[512,128]{1,0:T(8,128)(2,1)S(1)} collective-permute-done((bf16[512,128]{1,0:T(8,128)(2,1)}, bf16[512,128]{1,0:T(8,128)(2,1)S(1)}, u32[]{:S(2)}, u32[]{:S(2)}) %collective-permute-start) | collective-permute-done | bytes 131104 | tf_op jit(solution)/shard_map/ppermute | solution.py:92
  19.1 0.0 copy-start.4
  19.1 0.0 copy-done.1
  19.1 0.0 copy-done.2
  19.1 0.0 copy-done.3
  19.2 0.6 copy-done.4
  19.8 32.6 %attn_grads.1 = (bf16[512,512]{1,0:T(8,128)(2,1)}, f32[2560,128]{1,0:T(8,128)}) custom-call(bf16[512,512]{1,0:T(8,128)(2,1)} %bitcast.34, bf16[512,512]{1,0:T(8,128)(2,1)} %bitcast.35, bf16[512,128]{1,0:T(8,128)(2,1)} %bitcast.40, bf16[512,128]{1,0:T(8,128)(2,1)} %copy-done.4, bf16[512,128]{1,0:T(8,128)(2,1)} %copy-done.3, bf16[512,128]{1,0:T(8,128)(2,1)} %copy-done.2, ...), custom_call_target="tpu_custom_call" | custom-call | tf_op jit(solution)/shard_map/attn_grads/pallas_call | solution.py:81
  52.4 0.0 copy-start
  52.4 1.2 %dynamic-slice_bitcast_fusion = f32[5,256,128]{2,1,0:T(8,128)S(1)} fusion(f32[5,2,256,128]{3,2,1,0:T(8,128)} %bitcast.32, s32[]{:T(128)S(6)} %select_n.8), kind=kLoop, calls=%fused_computation.1 | loop fusion | bytes 1310724 | tf_op jit(solution)/shard_map/jit(dynamic_index_in_dim)/squeeze | solution.py:106
  53.7 1.3 %collective-permute-start.4 = (f32[5,256,128]{2,1,0:T(8,128)S(1)}, f32[5,256,128]{2,1,0:T(8,128)S(1)}, u32[]{:S(2)}, u32[]{:S(2)}) collective-permute-start(f32[5,256,128]{2,1,0:T(8,128)S(1)} %dynamic-slice_bitcast_fusion), channel_id=1, source_target_pairs={{0,1},{1,0},{2,3},{3,2},{4,5},{5,4},{6,7},{7,6},{8,9},{9,8},{10,11... | collective-permute-start | bytes 1966088 | tf_op jit(solution)/shard_map/ppermute | solution.py:92
  54.9 1.7 %collective-permute-done.4 = f32[5,256,128]{2,1,0:T(8,128)S(1)} collective-permute-done((f32[5,256,128]{2,1,0:T(8,128)S(1)}, f32[5,256,128]{2,1,0:T(8,128)S(1)}, u32[]{:S(2)}, u32[]{:S(2)}) %collective-permute-start.4) | collective-permute-done | bytes 655392 | tf_op jit(solution)/shard_map/ppermute | solution.py:92
  56.7 0.0 copy-done
  56.7 0.1 fusion.5
  56.8 3.4 %collective-permute-start.5 = (bf16[256,128]{1,0:T(8,128)(2,1)S(1)}, bf16[256,128]{1,0:T(8,128)(2,1)S(1)}, u32[]{:S(2)}, u32[]{:S(2)}) collective-permute-start(bf16[256,128]{1,0:T(8,128)(2,1)S(1)} %get-tuple-element.8), channel_id=1, source_target_pairs={{0,32},{16,48},{32,64},{48,80},{64,96},{80,112},{96,128},{112,144}... | collective-permute-start | bytes 196616 | tf_op jit(solution)/shard_map/ppermute | solution.py:92
  60.2 3.0 %collective-permute-start.8 = (bf16[256,128]{1,0:T(8,128)(2,1)S(1)}, bf16[256,128]{1,0:T(8,128)(2,1)S(1)}, u32[]{:S(2)}, u32[]{:S(2)}) collective-permute-start(bf16[256,128]{1,0:T(8,128)(2,1)S(1)} %get-tuple-element.9), channel_id=1, source_target_pairs={{0,12},{2,14},{4,0},{6,2},{8,4},{10,6},{12,8},{14,10},{1,13},{3,15... | collective-permute-start | bytes 196616 | tf_op jit(solution)/shard_map/ppermute | solution.py:92
  63.2 0.0 collective-permute-start.7
  63.2 4.2 %collective-permute-start.6 = (bf16[256,128]{1,0:T(8,128)(2,1)S(1)}, bf16[256,128]{1,0:T(8,128)(2,1)S(1)}, u32[]{:S(2)}, u32[]{:S(2)}) collective-permute-start(bf16[256,128]{1,0:T(8,128)(2,1)S(1)} %get-tuple-element.11), channel_id=1, source_target_pairs={{0,224},{16,240},{32,0},{48,16},{64,32},{80,48},{96,64},{112,80},{... | collective-permute-start | bytes 196616 | tf_op jit(solution)/shard_map/ppermute | solution.py:92
  67.4 0.0 collective-permute-done.5
  67.4 0.0 collective-permute-done.8
  67.4 1.3 %collective-permute-done.7 = bf16[256,128]{1,0:T(8,128)(2,1)S(1)} collective-permute-done((bf16[256,128]{1,0:T(8,128)(2,1)S(1)}, bf16[256,128]{1,0:T(8,128)(2,1)S(1)}, u32[]{:S(2)}, u32[]{:S(2)}) %collective-permute-start.7) | collective-permute-done | bytes 65568 | tf_op jit(solution)/shard_map/ppermute | solution.py:92
  68.7 0.0 collective-permute-done.6
  68.7 0.7 %fusion.4 = f32[1,1,256,128]{3,2,1,0:T(8,128)} fusion(f32[5,256,128]{2,1,0:T(8,128)S(1)} %get-tuple-element.7, bf16[256,128]{1,0:T(8,128)(2,1)S(1)} %collective-permute-done.8, bf16[256,128]{1,0:T(8,128)(2,1)S(1)} %collective-permute-done.7, bf16[256,128]{1,0:T(8,128)(2,1)S(1)} %collective-permute-done.6, bf16[256,128]{1,0:T(8,128)(2,1)S(1)} %collective-permute-done.5), kind=kLoop, calls=%fused_computation.7 | loop fusion | flops 262144 | bytes 524288 | tf_op jit(solution)/shard_map/broadcast_in_dim | solution.py:112
  (1 shorter events, 0.0 us)
Async XLA Ops:
  0.6 13.4 %collective-permute-start.3 = (bf16[512,128]{1,0:T(8,128)(2,1)}, bf16[512,128]{1,0:T(8,128)(2,1)S(1)}, u32[]{:S(2)}, u32[]{:S(2)}) collective-permute-start(bf16[512,128]{1,0:T(8,128)(2,1)} %bitcast.36), channel_id=1, source_target_pairs={{0,4},{2,6},{4,8},{6,10},{8,12},{10,14},{12,0},{14,2},{1,5},{3,7},... | collective-permute-start | bytes 393224 | tf_op jit(solution)/shard_map/ppermute | solution.py:92
  4.3 9.8 %collective-permute-start.2 = (bf16[512,128]{1,0:T(8,128)(2,1)}, bf16[512,128]{1,0:T(8,128)(2,1)S(1)}, u32[]{:S(2)}, u32[]{:S(2)}) collective-permute-start(bf16[512,128]{1,0:T(8,128)(2,1)} %bitcast.37), channel_id=1, source_target_pairs={{0,12},{2,14},{4,0},{6,2},{8,4},{10,6},{12,8},{14,10},{1,13},{3,15... | collective-permute-start | bytes 393224 | tf_op jit(solution)/shard_map/ppermute | solution.py:92
  5.4 11.6 %collective-permute-start.1 = (bf16[512,128]{1,0:T(8,128)(2,1)}, bf16[512,128]{1,0:T(8,128)(2,1)S(1)}, u32[]{:S(2)}, u32[]{:S(2)}) collective-permute-start(bf16[512,128]{1,0:T(8,128)(2,1)} %bitcast.38), channel_id=1, source_target_pairs={{0,32},{16,48},{32,64},{48,80},{64,96},{80,112},{96,128},{112,144}... | collective-permute-start | bytes 393224 | tf_op jit(solution)/shard_map/ppermute | solution.py:92
  8.4 10.8 %collective-permute-start = (bf16[512,128]{1,0:T(8,128)(2,1)}, bf16[512,128]{1,0:T(8,128)(2,1)S(1)}, u32[]{:S(2)}, u32[]{:S(2)}) collective-permute-start(bf16[512,128]{1,0:T(8,128)(2,1)} %bitcast.39), channel_id=1, source_target_pairs={{0,224},{16,240},{32,0},{48,16},{64,32},{80,48},{96,64},{112,80},{... | collective-permute-start | bytes 393224 | tf_op jit(solution)/shard_map/ppermute | solution.py:92
  14.1 5.1 %copy-start.1 = (bf16[512,128]{1,0:T(8,128)(2,1)}, bf16[512,128]{1,0:T(8,128)(2,1)S(1)}, u32[]{:S(2)}) copy-start(bf16[512,128]{1,0:T(8,128)(2,1)S(1)} %collective-permute-done.3.rest_4_) | copy-start | bytes 393220
  14.1 5.1 %copy-start.2 = (bf16[512,128]{1,0:T(8,128)(2,1)}, bf16[512,128]{1,0:T(8,128)(2,1)S(1)}, u32[]{:S(2)}) copy-start(bf16[512,128]{1,0:T(8,128)(2,1)S(1)} %collective-permute-done.2.rest_3_) | copy-start | bytes 393220
  17.0 2.1 %copy-start.3 = (bf16[512,128]{1,0:T(8,128)(2,1)}, bf16[512,128]{1,0:T(8,128)(2,1)S(1)}, u32[]{:S(2)}) copy-start(bf16[512,128]{1,0:T(8,128)(2,1)S(1)} %collective-permute-done.1.rest_2_) | copy-start | bytes 393220
  19.1 0.7 copy-start.4
  52.4 4.2 %copy-start = (f32[2560,128]{1,0:T(8,128)S(1)}, f32[2560,128]{1,0:T(8,128)}, u32[]{:S(2)}) copy-start(f32[2560,128]{1,0:T(8,128)} %get-tuple-element.5) | copy-start | bytes 3932164
  53.7 3.0 %collective-permute-start.4 = (f32[5,256,128]{2,1,0:T(8,128)S(1)}, f32[5,256,128]{2,1,0:T(8,128)S(1)}, u32[]{:S(2)}, u32[]{:S(2)}) collective-permute-start(f32[5,256,128]{2,1,0:T(8,128)S(1)} %dynamic-slice_bitcast_fusion), channel_id=1, source_target_pairs={{0,1},{1,0},{2,3},{3,2},{4,5},{5,4},{6,7},{7,6},{8,9},{9,8},{10,11... | collective-permute-start | bytes 1966088 | tf_op jit(solution)/shard_map/ppermute | solution.py:92
  56.8 10.5 %collective-permute-start.5 = (bf16[256,128]{1,0:T(8,128)(2,1)S(1)}, bf16[256,128]{1,0:T(8,128)(2,1)S(1)}, u32[]{:S(2)}, u32[]{:S(2)}) collective-permute-start(bf16[256,128]{1,0:T(8,128)(2,1)S(1)} %get-tuple-element.8), channel_id=1, source_target_pairs={{0,32},{16,48},{32,64},{48,80},{64,96},{80,112},{96,128},{112,144}... | collective-permute-start | bytes 196616 | tf_op jit(solution)/shard_map/ppermute | solution.py:92
  60.2 7.2 %collective-permute-start.8 = (bf16[256,128]{1,0:T(8,128)(2,1)S(1)}, bf16[256,128]{1,0:T(8,128)(2,1)S(1)}, u32[]{:S(2)}, u32[]{:S(2)}) collective-permute-start(bf16[256,128]{1,0:T(8,128)(2,1)S(1)} %get-tuple-element.9), channel_id=1, source_target_pairs={{0,12},{2,14},{4,0},{6,2},{8,4},{10,6},{12,8},{14,10},{1,13},{3,15... | collective-permute-start | bytes 196616 | tf_op jit(solution)/shard_map/ppermute | solution.py:92
  63.2 5.5 %collective-permute-start.7 = (bf16[256,128]{1,0:T(8,128)(2,1)S(1)}, bf16[256,128]{1,0:T(8,128)(2,1)S(1)}, u32[]{:S(2)}, u32[]{:S(2)}) collective-permute-start(bf16[256,128]{1,0:T(8,128)(2,1)S(1)} %get-tuple-element.10), channel_id=1, source_target_pairs={{0,4},{2,6},{4,8},{6,10},{8,12},{10,14},{12,0},{14,2},{1,5},{3,7},... | collective-permute-start | bytes 196616 | tf_op jit(solution)/shard_map/ppermute | solution.py:92
  63.2 5.5 %collective-permute-start.6 = (bf16[256,128]{1,0:T(8,128)(2,1)S(1)}, bf16[256,128]{1,0:T(8,128)(2,1)S(1)}, u32[]{:S(2)}, u32[]{:S(2)}) collective-permute-start(bf16[256,128]{1,0:T(8,128)(2,1)S(1)} %get-tuple-element.11), channel_id=1, source_target_pairs={{0,224},{16,240},{32,0},{48,16},{64,32},{80,48},{96,64},{112,80},{... | collective-permute-start | bytes 196616 | tf_op jit(solution)/shard_map/ppermute | solution.py:92

commit v2 on v1

--- a/solution.py
+++ b/solution.py
@@ -8,9 +8,11 @@
 from jax.sharding import PartitionSpec as P
 HD=64
 CH=256
-def kernel(heads, tok, tiles, q_ref, d_ref, *rest):
-    kv_refs=rest[:tiles]; dq_ref, g_ref = rest[tiles:tiles+2]
-    qz, dz, kT, s_ref, dp_ref, e_ref, acc, dqt, w_ref, stat = rest[tiles+2:]
+def kernel(heads, tok, tiles, q_ref, d_ref, own_ref, ahead_ref, behind_ref, other_ref,
+           dq_ref, gown_ref, gmine_ref, glent_ref,
+           qz, dz, kT, s_ref, dp_ref, e_ref, acc, dqt, w_ref, stat):
+    kv_refs=[own_ref,ahead_ref,behind_ref,other_ref.at[0],other_ref.at[1]]
+    g_refs=[gown_ref,gmine_ref.at[0],gmine_ref.at[1],glent_ref.at[0],glent_ref.at[1]]
     per=tok//CH; nch=tiles*per
     scale=1.0/HD**0.5
     c2=1.4426950408889634*scale
@@ -39,8 +41,8 @@
         for c in range(nch):
             if do3:
                 e=e_ref[c]
-                t=(g8(dp_ref[c])-delta8[None]).astype(bf).reshape(CH,tok)
-                g=e*t
+                t=(g8(dp_ref[c])-delta8[None]).reshape(CH,tok)
+                g=(e.astype(f32)*t).astype(bf)
                 r=jnp.dot(jnp.concatenate([g,e],axis=1),w_ref[...],preferred_element_type=f32)
                 acc[c]+=r
                 dqa=dqa+jnp.dot(kT[:,c*CH:(c+1)*CH],g,preferred_element_type=f32)
@@ -73,43 +75,58 @@
     step(heads,False,False,True)
     dq_ref[...]=dqt[...].reshape(heads*HD,tok).T
     for c in range(nch):
-        g_ref[c*CH:(c+1)*CH,:]=acc[c]
-def attn_grads(q,d,kvs):
-    tok,w=q.shape; heads=w//HD; tiles=len(kvs); nch=tiles*tok//CH
+        g_refs[c//per][(c%per)*CH:(c%per+1)*CH,:]=acc[c]
+def attn_grads(q,d,own,ahead,behind,others):
+    tok,w=q.shape; heads=w//HD; tiles=5; nch=tiles*tok//CH
     f32=jnp.float32; bf=jnp.bfloat16
     V=pl.BlockSpec(memory_space=pltpu.VMEM)
     return pl.pallas_call(functools.partial(kernel,heads,tok,tiles),
-        out_shape=(jax.ShapeDtypeStruct((tok,w),bf),jax.ShapeDtypeStruct((tiles*tok,2*HD),f32)),
-        in_specs=[V]*(2+tiles),out_specs=(V,V),
+        out_shape=(jax.ShapeDtypeStruct((tok,w),bf),jax.ShapeDtypeStruct((tok,2*HD),f32),
+          jax.ShapeDtypeStruct((2,tok,2*HD),f32),jax.ShapeDtypeStruct((2,tok,2*HD),f32)),
+        in_specs=[V]*6,out_specs=(V,V,V,V),
         scratch_shapes=[pltpu.VMEM((heads,2*HD,tok),bf),pltpu.VMEM((heads,2*HD,tok),bf),pltpu.VMEM((HD,tiles*tok),bf),
           pltpu.VMEM((nch,CH,tok),f32),pltpu.VMEM((nch,CH,tok),f32),pltpu.VMEM((nch,CH,tok),bf),
           pltpu.VMEM((nch,CH,2*HD),f32),pltpu.VMEM((heads,HD,tok),bf),pltpu.VMEM((2*tok,2*HD),bf),pltpu.VMEM((3,8,tok),f32)],
-        compiler_params=pltpu.CompilerParams(vmem_limit_bytes=60*2**20),name="attn_grads")(q,d,*kvs)
+        compiler_params=pltpu.CompilerParams(vmem_limit_bytes=60*2**20),name="attn_grads")(q,d,own,ahead,behind,others)
 
 
-def shifted(array, axis, by):
-    peers = lax.axis_size(axis)
-    return lax.ppermute(array, axis, [(i, (i + by) % peers) for i in range(peers)])
+AXES = ("lat", "lon", "head")
 
 
-STEPS = (("lat", -2), ("lat", 2), ("lon", -2), ("lon", 2))
+def partnered(array):
+    return lax.ppermute(array, "head", [(0, 1), (1, 0)])
+
+
+def spread(array, by):
+    nlat, nlon = lax.axis_size("lat"), lax.axis_size("lon")
+    pairs = []
+    for i in range(nlat):
+        for j in range(nlon):
+            here = (i * nlon + j) * 2
+            pairs.append((here, (((i + by) % nlat) * nlon + j) * 2))
+            pairs.append((here + 1, (i * nlon + (j + by) % nlon) * 2 + 1))
+    return lax.ppermute(array, AXES, pairs)
 
 
 def local(queries, key_value, dout):
+    bf = jnp.bfloat16
+    f32 = jnp.float32
     tile = key_value[0, 0]
     tok = tile.shape[0]
-    near = [shifted(tile, axis, by) for axis, by in STEPS]
-    dquery, grads = attn_grads(queries[0, 0], dout[0, 0], [tile] + near)
-    halves = grads.reshape(5, 2, tok // 2, 2 * HD)
+    ahead = spread(tile, -2)
+    behind = spread(tile, 2)
+    others = partnered(jnp.stack([ahead, behind]))
+    dquery, own, mine, lent = attn_grads(
+        queries[0, 0], dout[0, 0], tile, ahead, behind, others
+    )
+    both = mine + partnered(lent)
+    back = spread(both[0].astype(bf), 2).astype(f32)
+    forth = spread(both[1].astype(bf), -2).astype(f32)
+    total = (own + back + forth).reshape(2, tok // 2, 2 * HD)
     me = lax.axis_index("head")
-    keep = lax.dynamic_index_in_dim(halves, me, 1, keepdims=False)
-    send = lax.dynamic_index_in_dim(halves, 1 - me, 1, keepdims=False)
-    both = keep + shifted(send, "head", 1)
-    total = both[0]
-    for index, (axis, by) in enumerate(STEPS):
-        back = shifted(both[1 + index].astype(jnp.bfloat16), axis, -by)
-        total = total + back.astype(jnp.float32)
-    return dquery[None, None], total[None, None]
+    keep = lax.dynamic_index_in_dim(total, me, 0, keepdims=False)
+    send = lax.dynamic_index_in_dim(total, 1 - me, 0, keepdims=False)
+    return dquery[None, None], (keep + partnered(send))[None, None]
 
 
 def solution(mesh):

time: 70.1 us -> 72.2 us (1.030)
  waiting for transfers between devices: 8.13 us -> 14.8 us
  starting transfers between devices: 25.2 us -> 19.8 us
  other arithmetic: 0.8 us -> 1.86 us
  Pallas kernels: 32.6 us -> 33.4 us
    ppermute x9 -> x7, waiting for transfers between devices: 8.13 us -> 14.8 us  [the longest x4 10.9 us: spread(): return lax.ppermute(array, AXES, pairs)]
    ppermute x9 -> x7, starting transfers between devices: 25.2 us -> 19.8 us  [the longest x3 11.2 us: partnered(): return lax.ppermute(array, 'head', [(0, 1), (1, 0)])]
    squeeze x1, local copies, waits for them, and re-layouts: 1.24 us -> 0.02 us  [local(): send = lax.dynamic_index_in_dim(total, 1 - me, 0, keepdims=False)]
    another operation x1 -> x2, other arithmetic: 0.1 us -> 1.15 us
    pallas_call x1, Pallas kernels: 32.6 us -> 33.4 us  [attn_grads(): pl.pallas_call(functools.partial(kernel, heads, tok, tiles), out_shape=(j...]
  transfers between devices with their start and end apart: 9 -> 7, of which waited for: 4 -> 7; matrix products, arithmetic and copies ran while one was open for 0% -> 0% of each run, Pallas kernels for 0% -> 0%
where the time goes in v2:
time: 72.2 us; the launch traced here: 72 us
  Pallas kernels  33.4 us (46%)
  starting transfers between devices  19.8 us (27%)
  waiting for transfers between devices  14.8 us (20%)
  other arithmetic  1.86 us (3%)
  local copies, waits for them, and re-layouts  1.37 us (2%)
    pallas_call x1, Pallas kernels, attn_grads(): pl.pallas_call(functools.partial(kernel, heads, tok, tiles), out_shape=(j...  33.4 us
    ppermute x3, starting transfers between devices, partnered(): return lax.ppermute(array, 'head', [(0, 1), (1, 0)])  11.2 us
    ppermute x4, waiting for transfers between devices, spread(): return lax.ppermute(array, AXES, pairs)  10.9 us
    ppermute x4, starting transfers between devices, spread(): return lax.ppermute(array, AXES, pairs)  8.6 us
    ppermute x3, waiting for transfers between devices, partnered(): return lax.ppermute(array, 'head', [(0, 1), (1, 0)])  3.9 us
  transfers between devices with their start and end apart: 7, of which 7 were waited for; matrix products, arithmetic and copies ran while one was open for 0% of the time, Pallas kernels for 0%

profile of v2, /device:TPU:1, one launch (start us, length us, event | category | flops | bytes accessed | tf_op | source)
XLA Modules:
  0.0 72.0 jit_solution(3295469435587571170)
XLA Ops:
  0.6 4.7 %collective-permute-start = (bf16[512,128]{1,0:T(8,128)(2,1)}, bf16[512,128]{1,0:T(8,128)(2,1)S(1)}, u32[]{:S(2)}, u32[]{:S(2)}) collective-permute-start(bf16[512,128]{1,0:T(8,128)(2,1)} %bitcast.25), channel_id=1, source_target_pairs={{0,224},{1,13},{2,226},{3,15},{4,228},{5,1},{6,230},{7,3},{8,232},... | collective-permute-start | bytes 393224 | tf_op jit(solution)/shard_map/ppermute | solution.py:108
  5.3 0.0 collective-permute-start.1
  5.3 2.3 %collective-permute-done.ahead_ref = bf16[512,128]{1,0:T(8,128)(2,1)S(1)} collective-permute-done((bf16[512,128]{1,0:T(8,128)(2,1)}, bf16[512,128]{1,0:T(8,128)(2,1)S(1)}, u32[]{:S(2)}, u32[]{:S(2)}) %collective-permute-start) | collective-permute-done | bytes 131104 | tf_op jit(solution)/shard_map/ppermute | solution.py:108
  7.5 0.0 copy-start
  7.5 4.2 %collective-permute-done.1.behind_ref = bf16[512,128]{1,0:T(8,128)(2,1)S(1)} collective-permute-done((bf16[512,128]{1,0:T(8,128)(2,1)}, bf16[512,128]{1,0:T(8,128)(2,1)S(1)}, u32[]{:S(2)}, u32[]{:S(2)}) %collective-permute-start.1) | collective-permute-done | bytes 131104 | tf_op jit(solution)/shard_map/ppermute | solution.py:108
  11.7 0.0 copy-start.1
  11.7 0.0 copy-done
  11.8 0.6 copy-done.1
  12.4 9.2 %collective-permute-start.2 = (bf16[2,512,128]{2,1,0:T(8,128)(2,1)S(1)}, bf16[2,512,128]{2,1,0:T(8,128)(2,1)S(1)}, u32[]{:S(2)}, u32[]{:S(2)}) collective-permute-start(bf16[2,512,128]{2,1,0:T(8,128)(2,1)S(1)} %pad_maximum_fusion), channel_id=1, source_target_pairs={{0,1},{1,0},{2,3},{3,2},{4,5},{5,4},{6,7},{7,6},{8,9},{9,8},{10,11... | collective-permute-start | bytes 786440 | tf_op jit(solution)/shard_map/ppermute | solution.py:97
  21.6 1.2 %collective-permute-done.2.other_ref = bf16[2,512,128]{2,1,0:T(8,128)(2,1)S(1)} collective-permute-done((bf16[2,512,128]{2,1,0:T(8,128)(2,1)S(1)}, bf16[2,512,128]{2,1,0:T(8,128)(2,1)S(1)}, u32[]{:S(2)}, u32[]{:S(2)}) %collective-permute-start.2) | collective-permute-done | bytes 262176 | tf_op jit(solution)/shard_map/ppermute | solution.py:97
  22.7 0.0 copy-start.3
  22.7 0.7 copy-done.3
  23.5 33.4 %attn_grads.1 = (bf16[512,512]{1,0:T(8,128)(2,1)}, f32[512,128]{1,0:T(8,128)}, f32[2,512,128]{2,1,0:T(8,128)}, f32[2,512,128]{2,1,0:T(8,128)}) custom-call(bf16[512,512]{1,0:T(8,128)(2,1)} %bitcast.21, bf16[512,512]{1,0:T(8,128)(2,1)} %bitcast.22, bf16[512,128]{1,0:T(8,128)(2,1)} %bitcast.27, bf16[512,128]{1,0:T(8,128)(2,1)} %copy-done, ...), custom_call_target="tpu_custom_call" | custom-call | tf_op jit(solution)/shard_map/attn_grads/pallas_call | solution.py:83
  56.9 0.4 collective-permute-start.3
  57.3 1.7 %collective-permute-done.3 = f32[2,512,128]{2,1,0:T(8,128)S(1)} collective-permute-done((f32[2,512,128]{2,1,0:T(8,128)}, f32[2,512,128]{2,1,0:T(8,128)S(1)}, u32[]{:S(2)}, u32[]{:S(2)}) %collective-permute-start.3) | collective-permute-done | bytes 524320 | tf_op jit(solution)/shard_map/ppermute | solution.py:97
  59.0 1.1 %add_convert_fusion = bf16[2,512,128]{2,1,0:T(8,128)(2,1)S(1)} fusion(f32[2,512,128]{2,1,0:T(8,128)} %get-tuple-element.8, f32[2,512,128]{2,1,0:T(8,128)S(1)} %collective-permute-done.3), kind=kLoop, calls=%fused_computation | loop fusion | flops 262144 | bytes 1310720 | tf_op jit(solution)/shard_map/convert.1
  60.1 0.0 copy-start.2
  60.2 2.8 %collective-permute-start.4 = (bf16[512,128]{1,0:T(8,128)(2,1)S(1)}, bf16[512,128]{1,0:T(8,128)(2,1)S(1)}, u32[]{:S(2)}, u32[]{:S(2)}) collective-permute-start(bf16[512,128]{1,0:T(8,128)(2,1)S(1)} %get-tuple-element.10), channel_id=1, source_target_pairs={{0,32},{1,5},{2,34},{3,7},{4,36},{5,9},{6,38},{7,11},{8,40},{9,13}... | collective-permute-start | bytes 393224 | tf_op jit(solution)/shard_map/ppermute | solution.py:108
  63.0 1.1 %collective-permute-start.5 = (bf16[512,128]{1,0:T(8,128)(2,1)S(1)}, bf16[512,128]{1,0:T(8,128)(2,1)S(1)}, u32[]{:S(2)}, u32[]{:S(2)}) collective-permute-start(bf16[512,128]{1,0:T(8,128)(2,1)S(1)} %get-tuple-element.11), channel_id=1, source_target_pairs={{0,224},{1,13},{2,226},{3,15},{4,228},{5,1},{6,230},{7,3},{8,232},... | collective-permute-start | bytes 393224 | tf_op jit(solution)/shard_map/ppermute | solution.py:108
  64.1 2.4 %collective-permute-done.4 = bf16[512,128]{1,0:T(8,128)(2,1)S(1)} collective-permute-done((bf16[512,128]{1,0:T(8,128)(2,1)S(1)}, bf16[512,128]{1,0:T(8,128)(2,1)S(1)}, u32[]{:S(2)}, u32[]{:S(2)}) %collective-permute-start.4) | collective-permute-done | bytes 131104 | tf_op jit(solution)/shard_map/ppermute | solution.py:108
  66.6 2.1 %collective-permute-done.5 = bf16[512,128]{1,0:T(8,128)(2,1)S(1)} collective-permute-done((bf16[512,128]{1,0:T(8,128)(2,1)S(1)}, bf16[512,128]{1,0:T(8,128)(2,1)S(1)}, u32[]{:S(2)}, u32[]{:S(2)}) %collective-permute-start.5) | collective-permute-done | bytes 131104 | tf_op jit(solution)/shard_map/ppermute | solution.py:108
  68.6 0.0 copy-done.2
  68.7 1.6 %collective-permute-start.6 = (f32[256,128]{1,0:T(8,128)S(1)}, f32[256,128]{1,0:T(8,128)S(1)}, u32[]{:S(2)}, u32[]{:S(2)}) collective-permute-start(f32[256,128]{1,0:T(8,128)S(1)} %dynamic-slice_bitcast_fusion), channel_id=1, source_target_pairs={{0,1},{1,0},{2,3},{3,2},{4,5},{5,4},{6,7},{7,6},{8,9},{9,8},{10,11... | collective-permute-start | bytes 393224 | tf_op jit(solution)/shard_map/ppermute | solution.py:97
  70.3 1.0 %collective-permute-done.6 = f32[256,128]{1,0:T(8,128)S(1)} collective-permute-done((f32[256,128]{1,0:T(8,128)S(1)}, f32[256,128]{1,0:T(8,128)S(1)}, u32[]{:S(2)}, u32[]{:S(2)}) %collective-permute-start.6) | collective-permute-done | bytes 131104 | tf_op jit(solution)/shard_map/ppermute | solution.py:97
  71.3 0.7 fusion
  (4 shorter events, 0.1 us)
Async XLA Ops:
  0.6 6.9 %collective-permute-start = (bf16[512,128]{1,0:T(8,128)(2,1)}, bf16[512,128]{1,0:T(8,128)(2,1)S(1)}, u32[]{:S(2)}, u32[]{:S(2)}) collective-permute-start(bf16[512,128]{1,0:T(8,128)(2,1)} %bitcast.25), channel_id=1, source_target_pairs={{0,224},{1,13},{2,226},{3,15},{4,228},{5,1},{6,230},{7,3},{8,232},... | collective-permute-start | bytes 393224 | tf_op jit(solution)/shard_map/ppermute | solution.py:108
  5.3 6.4 %collective-permute-start.1 = (bf16[512,128]{1,0:T(8,128)(2,1)}, bf16[512,128]{1,0:T(8,128)(2,1)S(1)}, u32[]{:S(2)}, u32[]{:S(2)}) collective-permute-start(bf16[512,128]{1,0:T(8,128)(2,1)} %bitcast.26), channel_id=1, source_target_pairs={{0,32},{1,5},{2,34},{3,7},{4,36},{5,9},{6,38},{7,11},{8,40},{9,13}... | collective-permute-start | bytes 393224 | tf_op jit(solution)/shard_map/ppermute | solution.py:108
  7.5 4.2 %copy-start = (bf16[512,128]{1,0:T(8,128)(2,1)}, bf16[512,128]{1,0:T(8,128)(2,1)S(1)}, u32[]{:S(2)}) copy-start(bf16[512,128]{1,0:T(8,128)(2,1)S(1)} %collective-permute-done.ahead_ref) | copy-start | bytes 393220
  11.7 0.6 copy-start.1
  12.4 10.4 %collective-permute-start.2 = (bf16[2,512,128]{2,1,0:T(8,128)(2,1)S(1)}, bf16[2,512,128]{2,1,0:T(8,128)(2,1)S(1)}, u32[]{:S(2)}, u32[]{:S(2)}) collective-permute-start(bf16[2,512,128]{2,1,0:T(8,128)(2,1)S(1)} %pad_maximum_fusion), channel_id=1, source_target_pairs={{0,1},{1,0},{2,3},{3,2},{4,5},{5,4},{6,7},{7,6},{8,9},{9,8},{10,11... | collective-permute-start | bytes 786440 | tf_op jit(solution)/shard_map/ppermute | solution.py:97
  22.7 0.7 copy-start.3
  56.9 2.1 %collective-permute-start.3 = (f32[2,512,128]{2,1,0:T(8,128)}, f32[2,512,128]{2,1,0:T(8,128)S(1)}, u32[]{:S(2)}, u32[]{:S(2)}) collective-permute-start(f32[2,512,128]{2,1,0:T(8,128)} %get-tuple-element.9), channel_id=1, source_target_pairs={{0,1},{1,0},{2,3},{3,2},{4,5},{5,4},{6,7},{7,6},{8,9},{9,8},{10,11... | collective-permute-start | bytes 1572872 | tf_op jit(solution)/shard_map/ppermute | solution.py:97
  60.1 8.5 %copy-start.2 = (f32[512,128]{1,0:T(8,128)S(1)}, f32[512,128]{1,0:T(8,128)}, u32[]{:S(2)}) copy-start(f32[512,128]{1,0:T(8,128)} %get-tuple-element.7) | copy-start | bytes 786436
  60.2 6.4 %collective-permute-start.4 = (bf16[512,128]{1,0:T(8,128)(2,1)S(1)}, bf16[512,128]{1,0:T(8,128)(2,1)S(1)}, u32[]{:S(2)}, u32[]{:S(2)}) collective-permute-start(bf16[512,128]{1,0:T(8,128)(2,1)S(1)} %get-tuple-element.10), channel_id=1, source_target_pairs={{0,32},{1,5},{2,34},{3,7},{4,36},{5,9},{6,38},{7,11},{8,40},{9,13}... | collective-permute-start | bytes 393224 | tf_op jit(solution)/shard_map/ppermute | solution.py:108
  63.0 5.6 %collective-permute-start.5 = (bf16[512,128]{1,0:T(8,128)(2,1)S(1)}, bf16[512,128]{1,0:T(8,128)(2,1)S(1)}, u32[]{:S(2)}, u32[]{:S(2)}) collective-permute-start(bf16[512,128]{1,0:T(8,128)(2,1)S(1)} %get-tuple-element.11), channel_id=1, source_target_pairs={{0,224},{1,13},{2,226},{3,15},{4,228},{5,1},{6,230},{7,3},{8,232},... | collective-permute-start | bytes 393224 | tf_op jit(solution)/shard_map/ppermute | solution.py:108
  68.7 2.6 %collective-permute-start.6 = (f32[256,128]{1,0:T(8,128)S(1)}, f32[256,128]{1,0:T(8,128)S(1)}, u32[]{:S(2)}, u32[]{:S(2)}) collective-permute-start(f32[256,128]{1,0:T(8,128)S(1)} %dynamic-slice_bitcast_fusion), channel_id=1, source_target_pairs={{0,1},{1,0},{2,3},{3,2},{4,5},{5,4},{6,7},{7,6},{8,9},{9,8},{10,11... | collective-permute-start | bytes 393224 | tf_op jit(solution)/shard_map/ppermute | solution.py:97
